TPU v7x, 32 devices: a whole 2x2x4 slice. The times are simulated.
32 devices in a mesh: chan: 16 (over z, x, core), tm: 2 (over y).
Axes of the slice: x: 2, y: 2, z: 4, core: 2. Of those that a mesh axis runs over, the one named last changes fastest.
Arguments:
- traces: bfloat16 [512, 4, 2048], P('chan', None, 'tm'), may hold values from -40 to 40
- delays: int32 [128, 512], P(None, 'chan'), may hold values from 0 to 1023
- offsets: int32 [4], P('tm'), may hold values from 0 to 2047
Outputs:
- brightness: float32 [4, 128, 256], P('tm', 'chan')
All inputs are finite; a program needn't handle non-finite values.
Results may differ from a plain program's by a relative error of at most 0.0048.
Values may be sent and summed in bfloat16 or wider, within the bound.
A program may use at most 64 MiB of HBM per device.

v0:
```python
import math

import jax
import jax.numpy as jnp
from jax import lax
from jax.sharding import PartitionSpec as P

SAMPLES = 2048
BAND = 512
FB = 128
TB = 256
BAND_LO = 128
DEC = 8


epsilon = 1e-06
full_turn = 2.0 * math.pi


def angle_grid(first_ids, second_ids):
    product = first_ids[:, None] * second_ids[None, :] % SAMPLES
    return product.astype(jnp.float32) * (full_turn / SAMPLES)


def forward_table(sample_ids):
    band_bins = BAND_LO + jnp.arange(BAND, dtype=jnp.int32)
    angles = angle_grid(sample_ids, band_bins)
    return jnp.concatenate([jnp.cos(angles), -jnp.sin(angles)], axis=1).astype(jnp.bfloat16)


def on_device(traces, delays, offsets):
    channels_dev, windows, half_len = traces.shape
    channels_all = channels_dev * lax.axis_size("chan")
    own_times = lax.axis_index("tm") * half_len + jnp.arange(half_len, dtype=jnp.int32)
    band_bins = BAND_LO + jnp.arange(BAND, dtype=jnp.int32)
    local_terms = jnp.dot(
        traces.reshape(-1, half_len), forward_table(own_times), preferred_element_type=jnp.float32
    )
    spectrum = lax.psum(local_terms, "tm")
    row_len = own_times.shape[0]
    spectrum = spectrum.astype(jnp.bfloat16)
    taper = jnp.sin(jnp.pi * (jnp.arange(BAND, dtype=jnp.float32) + 0.5) / BAND) ** 2
    weight = (2.0 * taper / SAMPLES)[:, None]
    back_angles = angle_grid(band_bins, own_times)
    upper = jnp.concatenate([weight * jnp.cos(back_angles), weight * jnp.sin(back_angles)], axis=1)
    lower = jnp.concatenate([-weight * jnp.sin(back_angles), weight * jnp.cos(back_angles)], axis=1)
    inverse = jnp.concatenate([upper, lower], axis=0).astype(jnp.bfloat16)
    analytic = jnp.dot(spectrum, inverse, preferred_element_type=jnp.float32)
    real_part = analytic[:, :row_len]
    imag_part = analytic[:, row_len:]
    energy = real_part * real_part + imag_part * imag_part
    energy_sum = jnp.sum(energy, axis=1).reshape(channels_dev, -1)
    env_bins = 1 + jnp.arange(FB, dtype=jnp.int32)
    env_angles = angle_grid(own_times, env_bins)
    envelope_table = jnp.concatenate([jnp.cos(env_angles), -jnp.sin(env_angles)], axis=1).astype(
        jnp.bfloat16
    )
    envelope_spectrum = jnp.dot(
        energy.astype(jnp.bfloat16), envelope_table, preferred_element_type=jnp.float32
    )
    envelope_spectrum = envelope_spectrum.reshape(channels_dev, -1, 2 * FB)
    envelope_spectrum, energy_sum = (
        lax.psum_scatter(envelope_spectrum, "tm", scatter_dimension=1, tiled=True),
        lax.psum_scatter(energy_sum, "tm", scatter_dimension=1, tiled=True),
    )
    kept_windows = envelope_spectrum.shape[1]
    factor = 1.0 / (math.sqrt(SAMPLES) * (energy_sum / SAMPLES + epsilon))
    normalized = (envelope_spectrum * factor[:, :, None]).astype(jnp.bfloat16)
    e_real = normalized[:, :, :FB]
    e_imag = normalized[:, :, FB:]
    real_block = jnp.concatenate([e_real, -e_imag], axis=0)
    imag_block = jnp.concatenate([e_imag, e_real], axis=0)
    spectra_pair = jnp.concatenate([real_block, imag_block], axis=1)
    node_rows = delays.shape[0] // lax.axis_size("chan")
    block_size = math.gcd(node_rows * lax.axis_size("chan"), 64)

    def one_block(block_index):
        delay_rows = lax.dynamic_slice_in_dim(delays, block_index * block_size, block_size, 0)
        product = delay_rows[:, :, None] * env_bins[None, None, :] % SAMPLES
        angles = product.astype(jnp.float32) * (full_turn / SAMPLES)
        phase = jnp.concatenate([jnp.cos(angles), jnp.sin(angles)], axis=1).astype(jnp.bfloat16)
        summed = jnp.einsum("ncf,cwf->nwf", phase, spectra_pair, preferred_element_type=jnp.float32)
        return summed.reshape(block_size, 2, kept_windows, FB)

    blocks = lax.map(
        one_block, jnp.arange(node_rows * lax.axis_size("chan") // block_size, dtype=jnp.int32)
    )
    stacks = lax.psum_scatter(
        blocks.reshape(node_rows * lax.axis_size("chan"), 2, kept_windows, FB),
        "chan",
        scatter_dimension=0,
        tiled=True,
    )
    out_times = offsets[:, None] + DEC * jnp.arange(TB, dtype=jnp.int32)[None, :]
    product = env_bins[None, :, None] * out_times[:, None, :] % SAMPLES
    out_angles = product.astype(jnp.float32) * (full_turn / SAMPLES)
    scale = 1.0 / math.sqrt(FB * channels_all)
    bright = jnp.einsum(
        "nwf,wfk->wnk", stacks[:, 0], jnp.cos(out_angles), precision=lax.Precision.HIGHEST
    )
    bright = bright - jnp.einsum(
        "nwf,wfk->wnk", stacks[:, 1], jnp.sin(out_angles), precision=lax.Precision.HIGHEST
    )
    return bright * scale


def solution(mesh):
    placed = (P("chan", None, "tm"), P(None, "chan"), P("tm"))
    return jax.shard_map(
        on_device, mesh=mesh, in_specs=placed, out_specs=P("tm", "chan", None), check_vma=False
    )
```

profile of v0, /device:TPU:0, one launch (start us, length us, event | category | flops | bytes accessed | tf_op | source)
XLA Modules:
  0.0 153.1 jit_solution(13436095608261437592)
XLA Ops:
  6.5 0.0 reduce-scatter.4.cloned.1.call-start
  6.6 0.0 copy-start.2
  6.6 1.0 reshape.83
  7.6 9.1 %cosine_convert_fusion.1 = (bf16[1024,512]{1,0:T(8,128)(2,1)S(1)}, bf16[1024,512]{1,0:T(8,128)(2,1)S(1)}) fusion(s32[512]{0:T(512)S(1)} %iota_add_fusion.2, s32[1024]{0:T(1024)S(1)} %iota_add_fusion.1), kind=kLoop, calls=%fused_computation.47 | loop fusion | flops 8912896 | bytes 2103296 | tf_op jit(solution)/shard_map/convert.10
  16.8 0.7 fusion.23
  17.5 18.6 %all-reduce.2 = bf16[128,1024]{0,1:T(8,128)(2,1)S(1)} all-reduce(f32[128,1024]{0,1:T(8,128)S(1)} %fusion.23), channel_id=1, replica_groups=mesh['chan'=16,'tm'=2] {'tm'}, use_global_device_ids=true, to_apply=%region_0.1 | all-reduce | flops 131072 | bytes 786432 | tf_op jit(solution)/shard_map/psum | solution.py:39
  36.2 0.0 copy-done.2
  36.2 2.5 %cosine_convert_fusion.2 = (bf16[1024,128]{1,0:T(8,128)(2,1)S(1)}, bf16[1024,128]{1,0:T(8,128)(2,1)S(1)}) fusion(s32[128]{0:T(128)S(1)} %iota_add_fusion.3, s32[1024]{0:T(1024)S(1)} %iota_add_fusion.1), kind=kLoop, calls=%fused_computation.68 | loop fusion | flops 2228224 | bytes 528896 | tf_op jit(solution)/shard_map/convert.2
  38.7 9.3 %multiply_convert_fusion.1 = (bf16[512,1024]{1,0:T(8,128)(2,1)S(1)}, bf16[512,1024]{1,0:T(8,128)(2,1)S(1)}, bf16[512,1024]{1,0:T(8,128)(2,1)S(1)}) fusion(s32[1024]{0:T(1024)S(1)} %iota_add_fusion.1, s32[512]{0:T(512)S(1)} %iota_add_fusion.2, f32[512]{0:T(512)S(1)} %get-tuple-element.138, f32[512]{0:T(512)S(1)} %get-tuple-element.139), kind=kLoop, calls=%fused_computation.44 | loop fusion | flops 10485760 | bytes 3155968 | tf_op jit(solution)/shard_map/convert.9
  48.0 0.7 fusion.5
  48.7 0.0 copy-start.3
  48.7 0.0 copy-start
  48.7 0.2 fusion.32
  49.0 0.7 copy.18
  49.7 0.0 reduce-scatter.4.cloned.1.call-update
  49.7 0.0 reduce-scatter.6.cloned.1.call-start
  49.8 0.2 fusion.46
  49.9 0.1 reshape.85
  50.0 7.2 %all-reduce = f32[32,4]{1,0:T(8,128)S(1)} all-reduce(f32[32,4]{1,0:T(8,128)S(1)} %reshape.85), channel_id=3, replica_groups=mesh['chan'=16,'tm'=2] {'tm'}, use_global_device_ids=true, to_apply=%region_3.4.clone | all-reduce | flops 128 | bytes 1024
  57.3 0.0 copy-done.3
  57.3 0.6 dynamic-slice
  58.5 0.1 constant_dynamic-slice_fusion.1
  58.6 0.1 copy.19
  58.7 1.9 %reduce-scatter.4.cloned.1.call-done = f32[32,2,256]{2,0,1:T(8,128)} async-done(((f32[32,4,256]{2,0,1:T(8,128)}), f32[32,2,256]{2,0,1:T(8,128)}) %reduce-scatter.4.cloned.1.call-update) | async-done | bytes 65552 | tf_op jit(solution)/shard_map/reduce_scatter | solution.py:63
  60.6 0.9 multiply_convert_fusion.3
  61.5 0.1 copy.21
  61.7 0.6 iota.47
  62.2 0.0 copy-done
  62.2 22.9 %while.13 = (s32[]{:T(128)}, f32[2,64,2,2,128]{4,1,0,3,2:T(8,128)S(1)}, s32[2]{0:T(128)}, s32[128,32]{0,1:T(8,128)S(1)}, bf16[64,4,128]{0,1,2:T(4,128)(2,1)S(1)}...) while((s32[]{:T(128)}, f32[2,64,2,2,128]{4,1,0,3,2:T(8,128)S(1)}, s32[2]{0:T(128)}, ...), condition=%wide.region_5.6_spmd.clone, body=%wide.region_4.5_spmd.clone.sunk | while | flops 10485894 | bytes 7054495 | solution.py:85
  62.2 1.3 dynamic_slice.19
  64.1 0.1 constant_dynamic-slice_fusion.3
  64.2 0.1 copy.31
  64.3 4.9 %cosine_convert_fusion.4 = (bf16[64,32,128]{2,1,0:T(8,128)(2,1)S(1)}, bf16[64,32,128]{2,1,0:T(8,128)(2,1)S(1)}) fusion(s32[128]{0:T(128)S(1)} %iota_add_fusion.5, s32[64,32]{1,0:T(8,128)S(1)} %copy.31), kind=kLoop, calls=%fused_computation.11.clone.1 | loop fusion | flops 4194304 | bytes 1057280 | tf_op jit(solution)/shard_map/convert
  69.2 0.1 pad_maximum_fusion.2
  69.3 3.0 %copy.32 = bf16[64,64,128]{1,0,2:T(8,128)(2,1)S(1)} copy(bf16[64,64,128]{2,1,0:T(8,128)(2,1)S(1)} %pad_maximum_fusion.2) | data formatting | bytes 2097152 | tf_op jit(solution)/shard_map/while/body/eval_jaxpr/concatenate | solution.py:81
  72.3 1.2 fusion.70
  73.4 0.2 copy.33
  73.7 1.3 dynamic_slice.19
  75.6 0.1 constant_dynamic-slice_fusion.3
  75.6 0.1 copy.31
  75.7 4.9 %cosine_convert_fusion.4 = (bf16[64,32,128]{2,1,0:T(8,128)(2,1)S(1)}, bf16[64,32,128]{2,1,0:T(8,128)(2,1)S(1)}) fusion(s32[128]{0:T(128)S(1)} %iota_add_fusion.5, s32[64,32]{1,0:T(8,128)S(1)} %copy.31), kind=kLoop, calls=%fused_computation.11.clone.1 | loop fusion | flops 4194304 | bytes 1057280 | tf_op jit(solution)/shard_map/convert
  80.6 0.1 pad_maximum_fusion.2
  80.7 3.0 %copy.32 = bf16[64,64,128]{1,0,2:T(8,128)(2,1)S(1)} copy(bf16[64,64,128]{2,1,0:T(8,128)(2,1)S(1)} %pad_maximum_fusion.2) | data formatting | bytes 2097152 | tf_op jit(solution)/shard_map/while/body/eval_jaxpr/concatenate | solution.py:81
  83.7 1.2 fusion.70
  84.9 0.2 copy.33
  85.1 0.0 copy-start.1
  85.1 0.7 copy-done.1
  85.8 0.0 reduce-scatter.6.cloned.1.call-update
  85.8 0.7 broadcast_add_fusion
  86.5 55.2 %reduce-scatter.6.cloned.1.call-done = f32[8,2,2,128]{3,0,2,1:T(8,128)} async-done(((f32[128,2,2,128]{3,0,2,1:T(8,128)}), f32[8,2,2,128]{3,0,2,1:T(8,128)}) %reduce-scatter.6.cloned.1.call-update) | async-done | bytes 16400 | tf_op jit(solution)/shard_map/reduce_scatter | solution.py:88
  141.7 2.0 %fusion.40 = f32[2,8,256]{2,1,0:T(8,128)S(1)} fusion(s32[2,256]{1,0:T(2,128)S(1)} %broadcast_add_fusion, s32[128]{0:T(128)} %copy-done.2, f32[8,2,2,128]{3,0,2,1:T(8,128)} %reduce-scatter.6.cloned.1.call-done), kind=kOutput, calls=%fused_computation.78 | convolution fusion | flops 7208960 | bytes 27136 | tf_op jit(solution)/shard_map/nwf,wfk->wnk/dot_general | solution.py:98
  143.7 2.6 %fusion.26 = f32[2,8,256]{2,1,0:T(8,128)} fusion(f32[2,8,256]{2,1,0:T(8,128)S(1)} %fusion.40, s32[2,256]{1,0:T(2,128)S(1)} %broadcast_add_fusion, s32[128]{0:T(128)} %copy-done.2, f32[8,2,2,128]{3,0,2,1:T(8,128)} %reduce-scatter.6.cloned.1.call-done), kind=kOutput, calls=%fused_computation.50 | convolution fusion | flops 7217152 | bytes 43520 | tf_op jit(solution)/shard_map/nwf,wfk->wnk/dot_general | solution.py:101
  (14 shorter events, 0.2 us)
Async XLA Ops:
  6.5 54.0 %reduce-scatter.4.cloned.1.call-start = ((), (), s32[]{:S(2)}) async-start(), calls=%async_computation.2 | async-start | bytes 196608 | tf_op jit(solution)/shard_map/reduce_scatter | solution.py:63
  6.6 29.6 %copy-start.2 = (s32[128]{0:T(128)}, s32[128]{0:T(128)S(1)}, u32[]{:S(2)}) copy-start(s32[128]{0:T(128)S(1)} %iota_add_fusion.3) | copy-start | bytes 1540
  48.7 8.6 %copy-start.3 = (u32[32]{0:T(128)S(1)}, u32[32]{0:T(128)}, u32[]{:S(2)}) copy-start(u32[32]{0:T(128)} %constant.138) | copy-start | bytes 388
  48.7 13.5 %copy-start = (s32[128,32]{0,1:T(8,128)S(1)}, s32[128,32]{0,1:T(8,128)}, u32[]{:S(2)}) copy-start(s32[128,32]{0,1:T(8,128)} %param.6) | copy-start | bytes 49156
  49.7 92.0 %reduce-scatter.6.cloned.1.call-start = ((), (), s32[]{:S(2)}) async-start(), calls=%async_computation.3 | async-start | bytes 278528 | tf_op jit(solution)/shard_map/reduce_scatter | solution.py:88
  85.1 0.7 copy-start.1
Sparse Core Ops, SparseCore 0:
  49.8 10.6 reduce-scatter.3
  85.9 55.7 reduce-scatter.5
where the time goes:
time: 153 us
  waiting for transfers between devices  57.1 us (37%)
  other arithmetic  32.7 us (21%)
  blocking collectives  25.8 us (17%)
  between operations  14.2 us (9%)
  local copies, waits for them, and re-layouts  13.2 us (9%)
  matrix products  8.6 us (6%)
    reduce_scatter x1, waiting for transfers between devices, on_device(): lax.psum_scatter(blocks.reshape(node_rows * lax.axis_size('chan'), 2, kep...  55.2 us
    another operation x5, other arithmetic  30.6 us
    psum x1, blocking collectives, on_device(): spectrum = lax.psum(local_terms, 'tm')  18.6 us
    unnamed x1, blocking collectives  7.22 us
    concatenate x2, local copies, waits for them, and re-layouts, one_block(): jnp.concatenate([jnp.cos(angles), jnp.sin(angles)], axis=1)  5.97 us
  transfers between devices with their start and end apart: 2, of which 2 were waited for; matrix products, arithmetic and copies ran while one was open for 1% of the time, Pallas kernels for 0%

commit v1 on v0

v1 whole, which is shorter than its diff:
```python
import functools
import math

import jax
import jax.numpy as jnp
from jax import lax
from jax.experimental import pallas as pl
from jax.experimental.pallas import tpu as pltpu
from jax.sharding import PartitionSpec as P

SAMPLES = 2048
BAND = 512
FB = 128
TB = 256
BAND_LO = 128
DEC = 8
STEP = 32
PAIR = 2

epsilon = 1e-06
full_turn = 2.0 * math.pi
MESH = pl.DeviceIdType.MESH


def cos_sin(index):
    quarter = SAMPLES // 4
    turn = (index + quarter // 2) >> 9
    x = (index - (turn << 9)).astype(jnp.float32) * (full_turn / SAMPLES)
    y = x * x
    s = x + x * y * (-1.6666654611e-1 + y * (8.3321608736e-3 + y * -1.9515295891e-4))
    c = 1.0 - 0.5 * y + y * y * (
        4.166664568298827e-2 + y * (-1.388731625493765e-3 + y * 2.443315711809948e-5)
    )
    odd = (turn & 1) != 0
    cos_part = jnp.where(odd, s, c)
    sin_part = jnp.where(odd, c, s)
    cos_out = jnp.where(((turn + 1) & 2) != 0, -cos_part, cos_part)
    sin_out = jnp.where((turn & 2) != 0, -sin_part, sin_part)
    return cos_out, sin_out


def parity_row(first, width):
    ids = first + lax.broadcasted_iota(jnp.int32, (1, width), 1)
    return (1 - 2 * (ids & 1)).astype(jnp.float32)


def kernel(
    n_chan, x_ref, d_ref, off_ref, out_ref,
    other, base_c, base_s, lead_c, lead_s, fwd, inv, env, phase_c, phase_s,
    nodes_d, turn_tab, spec, e_tab, send_buf, recv_buf,
    x_send, x_recv, send_sem, recv_sem,
):
    windows, chans, half = x_ref.shape
    kept = windows // 2
    rows = kept * chans
    nodes = d_ref.shape[1]
    node_rows = nodes // n_chan
    me = lax.axis_index("chan")
    tm = lax.axis_index("tm")
    partner = 1 - tm

    barrier = pltpu.get_barrier_semaphore()
    pl.semaphore_signal(barrier, inc=1, device_id={"tm": partner}, device_id_type=MESH)

    @pl.loop(1, n_chan)
    def _(step):
        pl.semaphore_signal(
            barrier, inc=1, device_id={"chan": lax.rem(me + step, n_chan)}, device_id_type=MESH
        )

    width = BAND + FB
    lane = lax.broadcasted_iota(jnp.int32, (STEP, width), 1)
    row = lax.broadcasted_iota(jnp.int32, (STEP, width), 0)
    freq = jnp.where(lane < BAND, lane + BAND_LO, lane - BAND + 1)
    c, s = cos_sin((freq * row) & (SAMPLES - 1))
    base_c[...] = c
    base_s[...] = s
    leads = half // STEP
    for q in range(width // 128):
        first = (BAND_LO if q * 128 < BAND else 1 - BAND) + q * 128
        ids = first + lax.broadcasted_iota(jnp.int32, (leads, 128), 1)
        leap = STEP * lax.broadcasted_iota(jnp.int32, (leads, 128), 0)
        c, s = cos_sin((ids * leap) & (SAMPLES - 1))
        lead_c[q] = c
        lead_s[q] = s

    taper_angle = math.pi * (lax.broadcasted_iota(jnp.int32, (1, BAND), 1).astype(jnp.float32) + 0.5) / BAND
    weight = 2.0 * jnp.sin(taper_angle) ** 2 / SAMPLES

    @pl.loop(0, half // STEP)
    def _(a):
        at = pl.ds(pl.multiple_of(a * STEP, STEP), STEP)
        for q in range(width // 128):
            cols = slice(q * 128, (q + 1) * 128)
            ca, sa = lead_c[q, pl.ds(a, 1), :], lead_s[q, pl.ds(a, 1), :]
            cb, sb = base_c[:, cols], base_s[:, cols]
            c = ca * cb - sa * sb
            s = sa * cb + ca * sb
            if q * 128 < BAND:
                g = weight[:, cols]
                high = slice(BAND + q * 128, BAND + (q + 1) * 128)
                fwd[at, cols] = c.astype(jnp.bfloat16)
                fwd[at, high] = (-s).astype(jnp.bfloat16)
                inv[at, cols] = (g * c).astype(jnp.bfloat16)
                inv[at, high] = (g * s).astype(jnp.bfloat16)
            else:
                low = slice(q * 128 - BAND, (q + 1) * 128 - BAND)
                high = slice(FB + low.start, FB + low.stop)
                env[at, low] = c.astype(jnp.bfloat16)
                env[at, high] = (-s).astype(jnp.bfloat16)

    pl.semaphore_wait(barrier, n_chan)
    exchange = pltpu.make_async_remote_copy(
        src_ref=x_ref.at[pl.ds(partner * kept, kept)],
        dst_ref=other,
        send_sem=x_send,
        recv_sem=x_recv,
        device_id={"tm": partner},
        device_id_type=MESH,
    )
    exchange.start()

    nodes_d[...] = d_ref[...].T
    block = PAIR * node_rows
    env_bins = 1 + lax.broadcasted_iota(jnp.int32, (block, FB), 1)

    @pl.loop(0, nodes // block)
    def _(b):
        at = pl.ds(pl.multiple_of(b * block, block), block)
        delay = nodes_d[at, :]
        for ch in range(chans):
            c, s = cos_sin((delay[:, ch : ch + 1] * env_bins) & (SAMPLES - 1))
            phase_c[ch, at, :] = c.astype(jnp.bfloat16)
            phase_s[ch, at, :] = s.astype(jnp.bfloat16)

    f_col = 1 + lax.broadcasted_iota(jnp.int32, (FB, TB), 0)
    k_row = lax.broadcasted_iota(jnp.int32, (FB, TB), 1)
    c, s = cos_sin((f_col * k_row * DEC) & (SAMPLES - 1))
    turn_tab[:FB, :] = c
    turn_tab[FB:, :] = -s

    exchange.wait()

    own = x_ref[pl.ds(tm * kept, kept)].reshape(rows, half)
    own_terms = jnp.dot(own, fwd[...], preferred_element_type=jnp.float32)
    other_terms = jnp.dot(other[...].reshape(rows, half), fwd[...], preferred_element_type=jnp.float32)
    band_sign = parity_row(BAND_LO, 2 * BAND)
    is_late = (lax.broadcasted_iota(jnp.int32, (1, 2 * BAND), 1) * 0 + tm) == 1
    own_sign = jnp.where(is_late, band_sign, 1.0)
    other_sign = jnp.where(is_late, 1.0, band_sign)
    total = (own_terms * own_sign + other_terms * other_sign).astype(jnp.bfloat16).astype(jnp.float32)
    re, im = total[:, :BAND], total[:, BAND:]
    sign = band_sign[:, :BAND]
    for at, value in enumerate((re, re * sign, im, im * sign)):
        spec[at * rows : (at + 1) * rows, :BAND] = value.astype(jnp.bfloat16)
    for at, value in enumerate((-im, -im * sign, re, re * sign)):
        spec[at * rows : (at + 1) * rows, BAND:] = value.astype(jnp.bfloat16)
    analytic = lax.dot_general(
        spec[...], inv[...], (((1,), (1,)), ((), ())), preferred_element_type=jnp.float32
    )
    real_part, imag_part = analytic[: 2 * rows], analytic[2 * rows :]
    energy = real_part * real_part + imag_part * imag_part
    sums = jnp.sum(energy, axis=1, keepdims=True)
    sums = sums[:rows] + sums[rows:]
    spread = jnp.dot(energy.astype(jnp.bfloat16), env[...], preferred_element_type=jnp.float32)
    spread = spread[:rows] + spread[rows:] * parity_row(1, 2 * FB)
    factor = 1.0 / (math.sqrt(SAMPLES) * (sums / SAMPLES + epsilon))
    e_tab[...] = (spread * factor).astype(jnp.bfloat16).astype(jnp.float32)

    pairs = n_chan // PAIR
    my_pair = me // PAIR

    def pair_at(step):
        return lax.rem(my_pair + 1 + step, pairs)

    def outgoing(dest):
        return pltpu.make_async_remote_copy(
            src_ref=send_buf.at[dest],
            dst_ref=recv_buf.at[me],
            send_sem=send_sem.at[dest],
            recv_sem=recv_sem.at[me],
            device_id={"chan": dest},
            device_id_type=MESH,
        )

    def send_pair(step):
        for side in range(PAIR):
            dest = pair_at(step) * PAIR + side

            @pl.when(dest != me)
            def _():
                outgoing(dest).start()

    @pl.loop(0, pairs)
    def _(step):
        pair = pair_at(step)
        at = pl.ds(pl.multiple_of(pair * block, block), block)
        acc = [[jnp.zeros((block, FB), jnp.float32) for _ in range(kept)] for _ in range(2)]
        for ch in range(chans):
            pc = phase_c[ch, at, :].astype(jnp.float32)
            ps = phase_s[ch, at, :].astype(jnp.float32)
            for w in range(kept):
                r = w * chans + ch
                er, ei = e_tab[r : r + 1, :FB], e_tab[r : r + 1, FB:]
                acc[0][w] = acc[0][w] + (pc * er - ps * ei)
                acc[1][w] = acc[1][w] + (pc * ei + ps * er)
        for side in range(PAIR):
            part = slice(side * node_rows, (side + 1) * node_rows)
            packed = jnp.concatenate([acc[p][w][part] for p in range(2) for w in range(kept)], axis=0)
            send_buf[pair * PAIR + side] = packed.astype(jnp.bfloat16)

        @pl.when(step > 0)
        def _():
            send_pair(step - 1)

    send_pair(pairs - 1)

    def incoming(source):
        return pltpu.make_async_remote_copy(
            src_ref=send_buf.at[source],
            dst_ref=recv_buf.at[source],
            send_sem=send_sem.at[source],
            recv_sem=recv_sem.at[source],
            device_id={"chan": source},
            device_id_type=MESH,
        )

    def add_in(step, stack):
        source = lax.rem(me + n_chan - step, n_chan)
        incoming(source).wait_recv()
        return stack + recv_buf[source].astype(jnp.float32)

    stack = lax.fori_loop(1, n_chan, add_in, send_buf[me].astype(jnp.float32))

    bins = 1 + lax.broadcasted_iota(jnp.int32, (1, FB), 1)
    turned = []
    for w in range(kept):
        c, s = cos_sin((bins * off_ref[w]) & (SAMPLES - 1))
        re = stack[w * node_rows : (w + 1) * node_rows]
        im = stack[(kept + w) * node_rows : (kept + w + 1) * node_rows]
        turned.append(jnp.concatenate([re * c - im * s, re * s + im * c], axis=1))
    bright = jnp.dot(
        jnp.concatenate(turned, axis=0), turn_tab[...],
        precision=lax.Precision.HIGHEST, preferred_element_type=jnp.float32,
    )
    scale = 1.0 / math.sqrt(FB * chans * n_chan)
    out_ref[...] = (bright * scale).reshape(kept, node_rows, TB)

    @pl.loop(1, n_chan)
    def _(step):
        outgoing(lax.rem(me + step, n_chan)).wait_send()


def solution(mesh):
    n_chan = mesh.shape["chan"]

    def on_device(traces, delays, offsets):
        chans, windows, half = traces.shape
        nodes = delays.shape[0]
        kept = offsets.shape[0]
        node_rows = nodes // n_chan
        by_window = jnp.transpose(traces, (1, 0, 2))
        vmem = pl.BlockSpec(memory_space=pltpu.VMEM)
        packed_rows = 2 * kept * node_rows
        return pl.pallas_call(
            functools.partial(kernel, n_chan),
            out_shape=jax.ShapeDtypeStruct((kept, node_rows, TB), jnp.float32),
            in_specs=[vmem, vmem, pl.BlockSpec(memory_space=pltpu.SMEM)],
            out_specs=vmem,
            scratch_shapes=[
                pltpu.VMEM((kept, chans, half), jnp.bfloat16),
                pltpu.VMEM((STEP, BAND + FB), jnp.float32),
                pltpu.VMEM((STEP, BAND + FB), jnp.float32),
                pltpu.VMEM(((BAND + FB) // 128, half // STEP, 128), jnp.float32),
                pltpu.VMEM(((BAND + FB) // 128, half // STEP, 128), jnp.float32),
                pltpu.VMEM((half, 2 * BAND), jnp.bfloat16),
                pltpu.VMEM((half, 2 * BAND), jnp.bfloat16),
                pltpu.VMEM((half, 2 * FB), jnp.bfloat16),
                pltpu.VMEM((chans, nodes, FB), jnp.bfloat16),
                pltpu.VMEM((chans, nodes, FB), jnp.bfloat16),
                pltpu.VMEM((nodes, chans), jnp.int32),
                pltpu.VMEM((2 * FB, TB), jnp.float32),
                pltpu.VMEM((4 * kept * chans, 2 * BAND), jnp.bfloat16),
                pltpu.VMEM((kept * chans, 2 * FB), jnp.float32),
                pltpu.VMEM((n_chan, packed_rows, FB), jnp.bfloat16),
                pltpu.VMEM((n_chan, packed_rows, FB), jnp.bfloat16),
                pltpu.SemaphoreType.DMA,
                pltpu.SemaphoreType.DMA,
                pltpu.SemaphoreType.DMA((n_chan,)),
                pltpu.SemaphoreType.DMA((n_chan,)),
            ],
            compiler_params=pltpu.CompilerParams(
                collective_id=0, has_side_effects=True, vmem_limit_bytes=56 * 1024 * 1024
            ),
        )(by_window, delays.T, offsets)

    placed = (P("chan", None, "tm"), P(None, "chan"), P("tm"))
    return jax.shard_map(
        on_device, mesh=mesh, in_specs=placed, out_specs=P("tm", "chan", None), check_vma=False
    )
```

time: 153 us -> 22.6 us (0.15)
  waiting for transfers between devices: 57.1 us -> 0 us
  other arithmetic: 32.7 us -> 0 us
  blocking collectives: 25.8 us -> 0 us
  Pallas kernels: 0 us -> 19.3 us
  between operations: 14.2 us -> 0.01 us
  local copies, waits for them, and re-layouts: 13.2 us -> 3.05 us
  matrix products: 8.6 us -> 0 us
    reduce_scatter x2 -> x0, waiting for transfers between devices: 57.1 us -> none  [the longest x1 55.2 us: on_device(): lax.psum_scatter(blocks.reshape(node_rows * lax.axis_size('chan'), 2, kep...]
    another operation x5 -> x0, other arithmetic: 30.6 us -> none
    pallas_call x0 -> x1, Pallas kernels: none -> 19.3 us  [on_device(): pl.pallas_call(functools.partial(kernel, n_chan), out_shape=jax.ShapeDtyp...]
    psum x1 -> x0, blocking collectives: 18.6 us -> none  [on_device(): spectrum = lax.psum(local_terms, 'tm')]
    dot_general x7 -> x0, matrix products: 8.6 us -> none  [the longest x1 2.59 us: on_device(): jnp.einsum('nwf,wfk->wnk', stacks[:, 1], jnp.sin(out_angles), precision=l...]
    unnamed x1 -> x0, blocking collectives: 7.22 us -> none
    concatenate x2 -> x0, local copies, waits for them, and re-layouts: 5.97 us -> none  [one_block(): jnp.concatenate([jnp.cos(angles), jnp.sin(angles)], axis=1)]
    dynamic_slice x6 -> x0, local copies, waits for them, and re-layouts: 2.88 us -> none  [the longest x2 2.56 us: on_device(): lax.map(one_block, jnp.arange(node_rows * lax.axis_size('chan') // block_...]
  transfers between devices with their start and end apart: 2 -> 0, of which waited for: 2 -> 0; matrix products, arithmetic and copies ran while one was open for 1% -> 0% of each run, Pallas kernels for 0% -> 0%
where the time goes in v1:
time: 22.6 us; the launch traced here: 22.3 us
  Pallas kernels  19.3 us (85%)
  local copies, waits for them, and re-layouts  3.05 us (13%)
    pallas_call x1, Pallas kernels, on_device(): pl.pallas_call(functools.partial(kernel, n_chan), out_shape=jax.ShapeDtyp...  19.3 us
    unnamed x2, local copies, waits for them, and re-layouts  3.05 us

profile of v1, /device:TPU:0, one launch (start us, length us, event | category | flops | bytes accessed | tf_op | source)
XLA Modules:
  0.0 22.3 jit_solution(14320695233983375599)
XLA Ops:
  0.0 1.7 %copy.6 = bf16[32,4,1024]{2,0,1:T(8,128)(2,1)} copy(bf16[32,4,1024]{2,1,0:T(4,128)(2,1)} %param.3) | data formatting | bytes 524288 | tf_op args[0]
  1.7 19.3 %shard_map.37 = f32[2,8,256]{2,1,0:T(8,128)} custom-call(bf16[4,32,1024]{2,1,0:T(8,128)(2,1)} %bitcast.4, s32[32,128]{1,0:T(8,128)} %bitcast.5, s32[2]{0:T(128)} %off_ref.1), custom_call_target="tpu_custom_call" | custom-call | tf_op jit(solution)/shard_map/pallas_call | solution.py:265
  21.0 1.3 %copy.8 = f32[2,8,256]{2,1,0:T(8,128)} copy(f32[2,8,256]{2,1,0:T(8,128)} %shard_map.37) | data formatting | bytes 32768

commit v2 on v1

--- a/solution.py
+++ b/solution.py
@@ -22,21 +22,36 @@
 MESH = pl.DeviceIdType.MESH
 
 
-def cos_sin(index):
-    quarter = SAMPLES // 4
-    turn = (index + quarter // 2) >> 9
-    x = (index - (turn << 9)).astype(jnp.float32) * (full_turn / SAMPLES)
+COS_TURN = (
+    0.9999999890590201, -19.739204499453688, 64.93911745988827, -85.45013953077586,
+    60.16763095018129, -25.96759924584206, 6.528658157862129,
+)
+SIN_TURN = (
+    6.283185302511498, -41.341700405316736, 81.60513138576982, -76.70301535347629,
+    42.02592698341473, -14.899846660399582, 3.2381375010236435,
+)
+
+
+def cos_sin(turns):
+    x = turns - jnp.round(turns)
     y = x * x
-    s = x + x * y * (-1.6666654611e-1 + y * (8.3321608736e-3 + y * -1.9515295891e-4))
-    c = 1.0 - 0.5 * y + y * y * (
-        4.166664568298827e-2 + y * (-1.388731625493765e-3 + y * 2.443315711809948e-5)
-    )
-    odd = (turn & 1) != 0
-    cos_part = jnp.where(odd, s, c)
-    sin_part = jnp.where(odd, c, s)
-    cos_out = jnp.where(((turn + 1) & 2) != 0, -cos_part, cos_part)
-    sin_out = jnp.where((turn & 2) != 0, -sin_part, sin_part)
-    return cos_out, sin_out
+    c, s = COS_TURN[-1], SIN_TURN[-1]
+    for c_next, s_next in zip(COS_TURN[-2::-1], SIN_TURN[-2::-1]):
+        c = c * y + c_next
+        s = s * y + s_next
+    return c, s * x
+
+
+def float_iota(shape, axis):
+    return lax.broadcasted_iota(jnp.int32, shape, axis).astype(jnp.float32)
+
+
+def bit_of(value, at):
+    return lax.rem(value // (1 << at), 2)
+
+
+def flip(value, at):
+    return value + (1 - 2 * bit_of(value, at)) * (1 << at)
 
 
 def parity_row(first, width):
@@ -47,8 +62,8 @@
 def kernel(
     n_chan, x_ref, d_ref, off_ref, out_ref,
     other, base_c, base_s, lead_c, lead_s, fwd, inv, env, phase_c, phase_s,
-    nodes_d, turn_tab, spec, e_tab, send_buf, recv_buf,
-    x_send, x_recv, send_sem, recv_sem,
+    nodes_d, turn_tab, turn_row, spec, e_tab, send_buf, recv_buf,
+    x_send, x_recv, send_sem, recv_sem, round_sem,
 ):
     windows, chans, half = x_ref.shape
     kept = windows // 2
@@ -59,33 +74,46 @@
     tm = lax.axis_index("tm")
     partner = 1 - tm
 
+    rounds = n_chan.bit_length() - 1
     barrier = pltpu.get_barrier_semaphore()
     pl.semaphore_signal(barrier, inc=1, device_id={"tm": partner}, device_id_type=MESH)
-
-    @pl.loop(1, n_chan)
-    def _(step):
-        pl.semaphore_signal(
-            barrier, inc=1, device_id={"chan": lax.rem(me + step, n_chan)}, device_id_type=MESH
-        )
+    for r in range(rounds):
+        pl.semaphore_signal(barrier, inc=1, device_id={"chan": flip(me, r)}, device_id_type=MESH)
+
+    def tell(r):
+        if r < rounds:
+            pl.semaphore_signal(round_sem.at[r], inc=1, device_id={"chan": flip(me, r)}, device_id_type=MESH)
+
+    def hear(r):
+        if r < rounds:
+            pl.semaphore_wait(round_sem.at[r], 1)
+            tell(r + 1)
 
     width = BAND + FB
-    lane = lax.broadcasted_iota(jnp.int32, (STEP, width), 1)
-    row = lax.broadcasted_iota(jnp.int32, (STEP, width), 0)
-    freq = jnp.where(lane < BAND, lane + BAND_LO, lane - BAND + 1)
-    c, s = cos_sin((freq * row) & (SAMPLES - 1))
-    base_c[...] = c
-    base_s[...] = s
     leads = half // STEP
+    unit = 1.0 / SAMPLES
     for q in range(width // 128):
+        cols = slice(q * 128, (q + 1) * 128)
         first = (BAND_LO if q * 128 < BAND else 1 - BAND) + q * 128
-        ids = first + lax.broadcasted_iota(jnp.int32, (leads, 128), 1)
-        leap = STEP * lax.broadcasted_iota(jnp.int32, (leads, 128), 0)
-        c, s = cos_sin((ids * leap) & (SAMPLES - 1))
-        lead_c[q] = c
-        lead_s[q] = s
+        freq = (float_iota((1, 128), 1) + first) * unit
+        base_c[:, cols], base_s[:, cols] = cos_sin(float_iota((STEP, 128), 0) * freq)
+        lead_c[q], lead_s[q] = cos_sin(float_iota((leads, 128), 0) * (freq * STEP))
 
     taper_angle = math.pi * (lax.broadcasted_iota(jnp.int32, (1, BAND), 1).astype(jnp.float32) + 0.5) / BAND
     weight = 2.0 * jnp.sin(taper_angle) ** 2 / SAMPLES
+
+    pl.semaphore_wait(barrier, rounds + 1)
+    exchange = pltpu.make_async_remote_copy(
+        src_ref=x_ref.at[pl.ds(partner * kept, kept)],
+        dst_ref=other,
+        send_sem=x_send,
+        recv_sem=x_recv,
+        device_id={"tm": partner},
+        device_id_type=MESH,
+    )
+    exchange.start()
+
+    tell(0)
 
     @pl.loop(0, half // STEP)
     def _(a):
@@ -109,40 +137,33 @@
                 env[at, low] = c.astype(jnp.bfloat16)
                 env[at, high] = (-s).astype(jnp.bfloat16)
 
-    pl.semaphore_wait(barrier, n_chan)
-    exchange = pltpu.make_async_remote_copy(
-        src_ref=x_ref.at[pl.ds(partner * kept, kept)],
-        dst_ref=other,
-        send_sem=x_send,
-        recv_sem=x_recv,
-        device_id={"tm": partner},
-        device_id_type=MESH,
-    )
-    exchange.start()
-
-    nodes_d[...] = d_ref[...].T
+    hear(0)
+
+    nodes_d[...] = (d_ref[...].astype(jnp.float32) * unit).T
     block = PAIR * node_rows
-    env_bins = 1 + lax.broadcasted_iota(jnp.int32, (block, FB), 1)
+    env_bins = 1.0 + float_iota((1, FB), 1)
 
     @pl.loop(0, nodes // block)
     def _(b):
         at = pl.ds(pl.multiple_of(b * block, block), block)
         delay = nodes_d[at, :]
         for ch in range(chans):
-            c, s = cos_sin((delay[:, ch : ch + 1] * env_bins) & (SAMPLES - 1))
+            c, s = cos_sin(delay[:, ch : ch + 1] * env_bins)
             phase_c[ch, at, :] = c.astype(jnp.bfloat16)
             phase_s[ch, at, :] = s.astype(jnp.bfloat16)
 
-    f_col = 1 + lax.broadcasted_iota(jnp.int32, (FB, TB), 0)
-    k_row = lax.broadcasted_iota(jnp.int32, (FB, TB), 1)
-    c, s = cos_sin((f_col * k_row * DEC) & (SAMPLES - 1))
+    hear(1)
+    c, s = cos_sin((1.0 + float_iota((FB, TB), 0)) * (float_iota((FB, TB), 1) * (DEC * unit)))
     turn_tab[:FB, :] = c
     turn_tab[FB:, :] = -s
-
-    exchange.wait()
+    for w in range(kept):
+        shift = off_ref[w].astype(jnp.float32) * unit
+        turn_row[w, :, :FB], turn_row[w, :, FB:] = cos_sin(env_bins * shift)
+    hear(2)
 
     own = x_ref[pl.ds(tm * kept, kept)].reshape(rows, half)
     own_terms = jnp.dot(own, fwd[...], preferred_element_type=jnp.float32)
+    exchange.wait()
     other_terms = jnp.dot(other[...].reshape(rows, half), fwd[...], preferred_element_type=jnp.float32)
     band_sign = parity_row(BAND_LO, 2 * BAND)
     is_late = (lax.broadcasted_iota(jnp.int32, (1, 2 * BAND), 1) * 0 + tm) == 1
@@ -167,11 +188,18 @@
     factor = 1.0 / (math.sqrt(SAMPLES) * (sums / SAMPLES + epsilon))
     e_tab[...] = (spread * factor).astype(jnp.bfloat16).astype(jnp.float32)
 
+    for r in range(3, rounds):
+        hear(r)
+
     pairs = n_chan // PAIR
     my_pair = me // PAIR
 
     def pair_at(step):
-        return lax.rem(my_pair + 1 + step, pairs)
+        mask = pairs - 1 - step
+        found = 0
+        for at in range(rounds - 1):
+            found = found + lax.rem(bit_of(my_pair, at) + bit_of(mask, at), 2) * (1 << at)
+        return found
 
     def outgoing(dest):
         return pltpu.make_async_remote_copy(
@@ -225,17 +253,21 @@
             device_id_type=MESH,
         )
 
-    def add_in(step, stack):
-        source = lax.rem(me + n_chan - step, n_chan)
+    def add_one(source, stack):
         incoming(source).wait_recv()
         return stack + recv_buf[source].astype(jnp.float32)
 
-    stack = lax.fori_loop(1, n_chan, add_in, send_buf[me].astype(jnp.float32))
-
-    bins = 1 + lax.broadcasted_iota(jnp.int32, (1, FB), 1)
+    def add_pair(step, stack):
+        for side in range(PAIR):
+            stack = add_one(pair_at(step) * PAIR + side, stack)
+        return stack
+
+    stack = lax.fori_loop(0, pairs - 1, add_pair, send_buf[me].astype(jnp.float32))
+    stack = add_one(flip(me, 0), stack)
+
     turned = []
     for w in range(kept):
-        c, s = cos_sin((bins * off_ref[w]) & (SAMPLES - 1))
+        c, s = turn_row[w, :, :FB], turn_row[w, :, FB:]
         re = stack[w * node_rows : (w + 1) * node_rows]
         im = stack[(kept + w) * node_rows : (kept + w + 1) * node_rows]
         turned.append(jnp.concatenate([re * c - im * s, re * s + im * c], axis=1))
@@ -278,8 +310,9 @@
                 pltpu.VMEM((half, 2 * FB), jnp.bfloat16),
                 pltpu.VMEM((chans, nodes, FB), jnp.bfloat16),
                 pltpu.VMEM((chans, nodes, FB), jnp.bfloat16),
-                pltpu.VMEM((nodes, chans), jnp.int32),
+                pltpu.VMEM((nodes, chans), jnp.float32),
                 pltpu.VMEM((2 * FB, TB), jnp.float32),
+                pltpu.VMEM((kept, 1, 2 * FB), jnp.float32),
                 pltpu.VMEM((4 * kept * chans, 2 * BAND), jnp.bfloat16),
                 pltpu.VMEM((kept * chans, 2 * FB), jnp.float32),
                 pltpu.VMEM((n_chan, packed_rows, FB), jnp.bfloat16),
@@ -288,9 +321,10 @@
                 pltpu.SemaphoreType.DMA,
                 pltpu.SemaphoreType.DMA((n_chan,)),
                 pltpu.SemaphoreType.DMA((n_chan,)),
+                pltpu.SemaphoreType.REGULAR((n_chan.bit_length() - 1,)),
             ],
             compiler_params=pltpu.CompilerParams(
-                collective_id=0, has_side_effects=True, vmem_limit_bytes=56 * 1024 * 1024
+                collective_id=0, has_side_effects=True, vmem_limit_bytes=16 * 1024 * 1024 + 4 * chans * nodes * FB
             ),
         )(by_window, delays.T, offsets)
 

time: 22.6 us -> 20.9 us (0.925)
  Pallas kernels: 19.3 us -> 18.5 us
  local copies, waits for them, and re-layouts: 3.05 us -> 2.3 us
    pallas_call x1, Pallas kernels: 19.3 us -> 18.5 us  [on_device(): pl.pallas_call(functools.partial(kernel, n_chan), out_shape=jax.ShapeDtyp...]
    unnamed x2 -> x6, local copies, waits for them, and re-layouts: 3.05 us -> 2.3 us
where the time goes in v2:
time: 20.9 us; the launch traced here: 20.8 us
  Pallas kernels  18.5 us (89%)
  local copies, waits for them, and re-layouts  2.3 us (11%)
    pallas_call x1, Pallas kernels, on_device(): pl.pallas_call(functools.partial(kernel, n_chan), out_shape=jax.ShapeDtyp...  18.5 us
    unnamed x6, local copies, waits for them, and re-layouts  2.3 us

profile of v2, /device:TPU:0, one launch (start us, length us, event | category | flops | bytes accessed | tf_op | source)
XLA Modules:
  0.0 20.8 jit_solution(5279745881026022759)
XLA Ops:
  0.0 0.0 copy-start
  0.0 1.0 %copy.6 = bf16[32,4,1024]{2,0,1:T(8,128)(2,1)S(1)} copy(bf16[32,4,1024]{2,1,0:T(4,128)(2,1)} %param.3) | data formatting | bytes 524288 | tf_op args[0]
  1.1 0.0 copy-start.1
  1.1 0.0 copy-done
  1.1 0.6 %copy-done.1 = s32[2]{0:T(128)S(1)} copy-done((s32[2]{0:T(128)S(1)}, s32[2]{0:T(128)}, u32[]{:S(2)}) %copy-start.1) | copy-done | bytes 32
  1.7 18.5 %shard_map.37 = f32[2,8,256]{2,1,0:T(8,128)S(1)} custom-call(bf16[4,32,1024]{2,1,0:T(8,128)(2,1)S(1)} %bitcast.4, s32[32,128]{1,0:T(8,128)S(1)} %bitcast.5, s32[2]{0:T(128)S(1)} %copy-done.1), custom_call_target="tpu_custom_call" | custom-call | tf_op jit(solution)/shard_map/pallas_call | solution.py:297
  20.2 0.6 %copy.8 = f32[2,8,256]{2,1,0:T(8,128)} copy(f32[2,8,256]{2,1,0:T(8,128)S(1)} %shard_map.37) | data formatting | bytes 32768
Async XLA Ops:
  0.0 1.1 %copy-start = (s32[128,32]{0,1:T(8,128)S(1)}, s32[128,32]{0,1:T(8,128)}, u32[]{:S(2)}) copy-start(s32[128,32]{0,1:T(8,128)} %param.4) | copy-start | bytes 49156
  1.1 0.7 %copy-start.1 = (s32[2]{0:T(128)S(1)}, s32[2]{0:T(128)}, u32[]{:S(2)}) copy-start(s32[2]{0:T(128)} %off_ref.1) | copy-start | bytes 28

commit v3 on v2

--- a/solution.py
+++ b/solution.py
@@ -60,10 +60,10 @@
 
 
 def kernel(
-    n_chan, x_ref, d_ref, off_ref, out_ref,
+    n_chan, x_ref, d_ref, off_hbm, out_ref,
     other, base_c, base_s, lead_c, lead_s, fwd, inv, env, phase_c, phase_s,
-    nodes_d, turn_tab, turn_row, spec, e_tab, send_buf, recv_buf,
-    x_send, x_recv, send_sem, recv_sem, round_sem,
+    nodes_d, turn_tab, turn_row, e_tab, send_buf, recv_buf,
+    off_ref, off_sem, x_send, x_recv, send_sem, recv_sem, round_sem,
 ):
     windows, chans, half = x_ref.shape
     kept = windows // 2
@@ -74,6 +74,9 @@
     tm = lax.axis_index("tm")
     partner = 1 - tm
 
+    offsets_in = pltpu.make_async_copy(off_hbm, off_ref, off_sem)
+    offsets_in.start()
+
     rounds = n_chan.bit_length() - 1
     barrier = pltpu.get_barrier_semaphore()
     pl.semaphore_signal(barrier, inc=1, device_id={"tm": partner}, device_id_type=MESH)
@@ -90,16 +93,23 @@
             tell(r + 1)
 
     width = BAND + FB
+    tiles = BAND // 128
+    side_tiles = tiles // 2
+    side_band = BAND // 2
     leads = half // STEP
     unit = 1.0 / SAMPLES
     for q in range(width // 128):
         cols = slice(q * 128, (q + 1) * 128)
-        first = (BAND_LO if q * 128 < BAND else 1 - BAND) + q * 128
-        freq = (float_iota((1, 128), 1) + first) * unit
+        if q < tiles:
+            freq = (2.0 * float_iota((1, 128), 1) + (BAND_LO + q % side_tiles * 256 + q // side_tiles)) * unit
+        else:
+            freq = (float_iota((1, 128), 1) + (1 + (q - tiles) * 128)) * unit
         base_c[:, cols], base_s[:, cols] = cos_sin(float_iota((STEP, 128), 0) * freq)
         lead_c[q], lead_s[q] = cos_sin(float_iota((leads, 128), 0) * (freq * STEP))
 
-    taper_angle = math.pi * (lax.broadcasted_iota(jnp.int32, (1, BAND), 1).astype(jnp.float32) + 0.5) / BAND
+    place = float_iota((1, side_band), 1) * 2.0
+    place = jnp.concatenate([place, place + 1.0], axis=1)
+    taper_angle = math.pi * (place + 0.5) / BAND
     weight = 2.0 * jnp.sin(taper_angle) ** 2 / SAMPLES
 
     pl.semaphore_wait(barrier, rounds + 1)
@@ -129,8 +139,9 @@
                 high = slice(BAND + q * 128, BAND + (q + 1) * 128)
                 fwd[at, cols] = c.astype(jnp.bfloat16)
                 fwd[at, high] = (-s).astype(jnp.bfloat16)
-                inv[at, cols] = (g * c).astype(jnp.bfloat16)
-                inv[at, high] = (g * s).astype(jnp.bfloat16)
+                to = q // side_tiles * BAND + q % side_tiles * 128
+                inv[at, to : to + 128] = (g * c).astype(jnp.bfloat16)
+                inv[at, to + side_band : to + side_band + 128] = (g * s).astype(jnp.bfloat16)
             else:
                 low = slice(q * 128 - BAND, (q + 1) * 128 - BAND)
                 high = slice(FB + low.start, FB + low.stop)
@@ -143,19 +154,31 @@
     block = PAIR * node_rows
     env_bins = 1.0 + float_iota((1, FB), 1)
 
-    @pl.loop(0, nodes // block)
-    def _(b):
-        at = pl.ds(pl.multiple_of(b * block, block), block)
+    pairs = n_chan // PAIR
+    ahead = (pairs + 1) // 2
+    my_pair = me // PAIR
+
+    def pair_at(step):
+        mask = pairs - 1 - step
+        found = 0
+        for at in range(rounds - 1):
+            found = found + lax.rem(bit_of(my_pair, at) + bit_of(mask, at), 2) * (1 << at)
+        return found
+
+    def phases(step):
+        at = pl.ds(pl.multiple_of(pair_at(step) * block, block), block)
         delay = nodes_d[at, :]
         for ch in range(chans):
             c, s = cos_sin(delay[:, ch : ch + 1] * env_bins)
             phase_c[ch, at, :] = c.astype(jnp.bfloat16)
             phase_s[ch, at, :] = s.astype(jnp.bfloat16)
 
+    pl.loop(0, ahead)(phases)
     hear(1)
     c, s = cos_sin((1.0 + float_iota((FB, TB), 0)) * (float_iota((FB, TB), 1) * (DEC * unit)))
     turn_tab[:FB, :] = c
     turn_tab[FB:, :] = -s
+    offsets_in.wait()
     for w in range(kept):
         shift = off_ref[w].astype(jnp.float32) * unit
         turn_row[w, :, :FB], turn_row[w, :, FB:] = cos_sin(env_bins * shift)
@@ -165,21 +188,29 @@
     own_terms = jnp.dot(own, fwd[...], preferred_element_type=jnp.float32)
     exchange.wait()
     other_terms = jnp.dot(other[...].reshape(rows, half), fwd[...], preferred_element_type=jnp.float32)
-    band_sign = parity_row(BAND_LO, 2 * BAND)
-    is_late = (lax.broadcasted_iota(jnp.int32, (1, 2 * BAND), 1) * 0 + tm) == 1
-    own_sign = jnp.where(is_late, band_sign, 1.0)
-    other_sign = jnp.where(is_late, 1.0, band_sign)
-    total = (own_terms * own_sign + other_terms * other_sign).astype(jnp.bfloat16).astype(jnp.float32)
-    re, im = total[:, :BAND], total[:, BAND:]
-    sign = band_sign[:, :BAND]
-    for at, value in enumerate((re, re * sign, im, im * sign)):
-        spec[at * rows : (at + 1) * rows, :BAND] = value.astype(jnp.bfloat16)
-    for at, value in enumerate((-im, -im * sign, re, re * sign)):
-        spec[at * rows : (at + 1) * rows, BAND:] = value.astype(jnp.bfloat16)
-    analytic = lax.dot_general(
-        spec[...], inv[...], (((1,), (1,)), ((), ())), preferred_element_type=jnp.float32
-    )
-    real_part, imag_part = analytic[: 2 * rows], analytic[2 * rows :]
+    late_sign = jnp.where((lax.broadcasted_iota(jnp.int32, (1, side_band), 1) * 0 + tm) == 1, -1.0, 1.0)
+
+    def spectrum(first, odd):
+        cols = slice(first, first + side_band)
+        mine, theirs = own_terms[:, cols], other_terms[:, cols]
+        both = (mine - theirs) * late_sign if odd else mine + theirs
+        return both.astype(jnp.bfloat16).astype(jnp.float32)
+
+    def analytic(odd):
+        re, im = spectrum(odd * side_band, odd), spectrum(BAND + odd * side_band, odd)
+        left = jnp.concatenate([re, im], axis=0)
+        right = jnp.concatenate([-im, re], axis=0)
+        return lax.dot_general(
+            jnp.concatenate([left, right], axis=1).astype(jnp.bfloat16),
+            inv[:, odd * BAND : (odd + 1) * BAND],
+            (((1,), (1,)), ((), ())),
+            preferred_element_type=jnp.float32,
+        )
+
+    even_part, odd_part = analytic(0), analytic(1)
+    early, late = even_part + odd_part, even_part - odd_part
+    real_part = jnp.concatenate([early[:rows], late[:rows]], axis=0)
+    imag_part = jnp.concatenate([early[rows:], late[rows:]], axis=0)
     energy = real_part * real_part + imag_part * imag_part
     sums = jnp.sum(energy, axis=1, keepdims=True)
     sums = sums[:rows] + sums[rows:]
@@ -190,16 +221,6 @@
 
     for r in range(3, rounds):
         hear(r)
-
-    pairs = n_chan // PAIR
-    my_pair = me // PAIR
-
-    def pair_at(step):
-        mask = pairs - 1 - step
-        found = 0
-        for at in range(rounds - 1):
-            found = found + lax.rem(bit_of(my_pair, at) + bit_of(mask, at), 2) * (1 << at)
-        return found
 
     def outgoing(dest):
         return pltpu.make_async_remote_copy(
@@ -221,6 +242,10 @@
 
     @pl.loop(0, pairs)
     def _(step):
+        @pl.when(step >= ahead)
+        def _():
+            phases(step)
+
         pair = pair_at(step)
         at = pl.ds(pl.multiple_of(pair * block, block), block)
         acc = [[jnp.zeros((block, FB), jnp.float32) for _ in range(kept)] for _ in range(2)]
@@ -297,7 +322,7 @@
         return pl.pallas_call(
             functools.partial(kernel, n_chan),
             out_shape=jax.ShapeDtypeStruct((kept, node_rows, TB), jnp.float32),
-            in_specs=[vmem, vmem, pl.BlockSpec(memory_space=pltpu.SMEM)],
+            in_specs=[vmem, vmem, pl.BlockSpec(memory_space=pltpu.HBM)],
             out_specs=vmem,
             scratch_shapes=[
                 pltpu.VMEM((kept, chans, half), jnp.bfloat16),
@@ -313,10 +338,11 @@
                 pltpu.VMEM((nodes, chans), jnp.float32),
                 pltpu.VMEM((2 * FB, TB), jnp.float32),
                 pltpu.VMEM((kept, 1, 2 * FB), jnp.float32),
-                pltpu.VMEM((4 * kept * chans, 2 * BAND), jnp.bfloat16),
                 pltpu.VMEM((kept * chans, 2 * FB), jnp.float32),
                 pltpu.VMEM((n_chan, packed_rows, FB), jnp.bfloat16),
                 pltpu.VMEM((n_chan, packed_rows, FB), jnp.bfloat16),
+                pltpu.SMEM((kept,), jnp.int32),
+                pltpu.SemaphoreType.DMA,
                 pltpu.SemaphoreType.DMA,
                 pltpu.SemaphoreType.DMA,
                 pltpu.SemaphoreType.DMA((n_chan,)),

time: 20.9 us -> 19.8 us (0.947)
  Pallas kernels: 18.5 us -> 17.3 us
    pallas_call x1, Pallas kernels: 18.5 us -> 17.3 us  [on_device(): pl.pallas_call(functools.partial(kernel, n_chan), out_shape=jax.ShapeDtyp...]
where the time goes in v3:
time: 19.8 us; the launch traced here: 19.6 us
  Pallas kernels  17.3 us (87%)
  local copies, waits for them, and re-layouts  2.3 us (12%)
    pallas_call x1, Pallas kernels, on_device(): pl.pallas_call(functools.partial(kernel, n_chan), out_shape=jax.ShapeDtyp...  17.3 us
    unnamed x6, local copies, waits for them, and re-layouts  2.3 us

profile of v3, /device:TPU:0, one launch (start us, length us, event | category | flops | bytes accessed | tf_op | source)
XLA Modules:
  0.0 19.6 jit_solution(13566808154795563866)
XLA Ops:
  0.0 0.0 copy-start
  0.0 1.0 %copy.6 = bf16[32,4,1024]{2,0,1:T(8,128)(2,1)S(1)} copy(bf16[32,4,1024]{2,1,0:T(4,128)(2,1)} %param.3) | data formatting | bytes 524288 | tf_op args[0]
  1.1 0.0 copy-start.1
  1.1 0.0 copy-done
  1.1 0.6 %copy-done.1 = s32[2]{0:T(128)S(1)} copy-done((s32[2]{0:T(128)S(1)}, s32[2]{0:T(128)}, u32[]{:S(2)}) %copy-start.1) | copy-done | bytes 32
  1.7 17.3 %shard_map.37 = f32[2,8,256]{2,1,0:T(8,128)S(1)} custom-call(bf16[4,32,1024]{2,1,0:T(8,128)(2,1)S(1)} %bitcast.4, s32[32,128]{1,0:T(8,128)S(1)} %bitcast.5, s32[2]{0:T(128)S(1)} %copy-done.1), custom_call_target="tpu_custom_call" | custom-call | tf_op jit(solution)/shard_map/pallas_call | solution.py:322
  19.0 0.6 %copy.8 = f32[2,8,256]{2,1,0:T(8,128)} copy(f32[2,8,256]{2,1,0:T(8,128)S(1)} %shard_map.37) | data formatting | bytes 32768
Async XLA Ops:
  0.0 1.1 %copy-start = (s32[128,32]{0,1:T(8,128)S(1)}, s32[128,32]{0,1:T(8,128)}, u32[]{:S(2)}) copy-start(s32[128,32]{0,1:T(8,128)} %param.4) | copy-start | bytes 49156
  1.1 0.7 %copy-start.1 = (s32[2]{0:T(128)S(1)}, s32[2]{0:T(128)}, u32[]{:S(2)}) copy-start(s32[2]{0:T(128)} %off_hbm.1) | copy-start | bytes 28

commit v4 on v3

--- a/solution.py
+++ b/solution.py
@@ -60,21 +60,25 @@
 
 
 def kernel(
-    n_chan, x_ref, d_ref, off_hbm, out_ref,
-    other, base_c, base_s, lead_c, lead_s, fwd, inv, env, phase_c, phase_s,
+    n_chan, x_hbm, d_hbm, off_hbm, out_ref,
+    x_ref, d_ref, other, all_rows, base_c, base_s, lead_c, lead_s, fwd, inv, env, phase_c, phase_s,
     nodes_d, turn_tab, turn_row, e_tab, send_buf, recv_buf,
-    off_ref, off_sem, x_send, x_recv, send_sem, recv_sem, round_sem,
+    off_ref, off_sem, x_sem, d_sem, x_send, x_recv, send_sem, recv_sem, round_sem,
 ):
-    windows, chans, half = x_ref.shape
+    chans, windows, half = x_hbm.shape
     kept = windows // 2
     rows = kept * chans
-    nodes = d_ref.shape[1]
+    nodes = d_hbm.shape[1]
     node_rows = nodes // n_chan
     me = lax.axis_index("chan")
     tm = lax.axis_index("tm")
     partner = 1 - tm
 
     offsets_in = pltpu.make_async_copy(off_hbm, off_ref, off_sem)
+    samples_in = pltpu.make_async_copy(x_hbm, x_ref, x_sem)
+    delays_in = pltpu.make_async_copy(d_hbm, d_ref, d_sem)
+    samples_in.start()
+    delays_in.start()
     offsets_in.start()
 
     rounds = n_chan.bit_length() - 1
@@ -114,7 +118,7 @@
 
     pl.semaphore_wait(barrier, rounds + 1)
     exchange = pltpu.make_async_remote_copy(
-        src_ref=x_ref.at[pl.ds(partner * kept, kept)],
+        src_ref=x_hbm,
         dst_ref=other,
         send_sem=x_send,
         recv_sem=x_recv,
@@ -150,6 +154,7 @@
 
     hear(0)
 
+    delays_in.wait()
     nodes_d[...] = (d_ref[...].astype(jnp.float32) * unit).T
     block = PAIR * node_rows
     env_bins = 1.0 + float_iota((1, FB), 1)
@@ -184,10 +189,24 @@
         turn_row[w, :, :FB], turn_row[w, :, FB:] = cos_sin(env_bins * shift)
     hear(2)
 
-    own = x_ref[pl.ds(tm * kept, kept)].reshape(rows, half)
-    own_terms = jnp.dot(own, fwd[...], preferred_element_type=jnp.float32)
+    def kept_terms(samples):
+        terms = jnp.dot(samples.reshape(chans * windows, half), fwd[...], preferred_element_type=jnp.float32)
+        cols = []
+        for q in range(2 * BAND // 128):
+            all_rows[q] = terms[:, q * 128 : (q + 1) * 128]
+            picked = []
+            for w in range(kept):
+                early = all_rows[q, pl.ds(w, chans, stride=windows), :]
+                late = all_rows[q, pl.ds(kept + w, chans, stride=windows), :]
+                picked.append(jnp.where(is_late, late, early))
+            cols.append(jnp.concatenate(picked, axis=0))
+        return jnp.concatenate(cols, axis=1)
+
+    is_late = (lax.broadcasted_iota(jnp.int32, (1, 128), 1) * 0 + tm) == 1
+    samples_in.wait()
+    own_terms = kept_terms(x_ref[...])
     exchange.wait()
-    other_terms = jnp.dot(other[...].reshape(rows, half), fwd[...], preferred_element_type=jnp.float32)
+    other_terms = kept_terms(other[...])
     late_sign = jnp.where((lax.broadcasted_iota(jnp.int32, (1, side_band), 1) * 0 + tm) == 1, -1.0, 1.0)
 
     def spectrum(first, odd):
@@ -316,16 +335,18 @@
         nodes = delays.shape[0]
         kept = offsets.shape[0]
         node_rows = nodes // n_chan
-        by_window = jnp.transpose(traces, (1, 0, 2))
         vmem = pl.BlockSpec(memory_space=pltpu.VMEM)
         packed_rows = 2 * kept * node_rows
         return pl.pallas_call(
             functools.partial(kernel, n_chan),
             out_shape=jax.ShapeDtypeStruct((kept, node_rows, TB), jnp.float32),
-            in_specs=[vmem, vmem, pl.BlockSpec(memory_space=pltpu.HBM)],
+            in_specs=[pl.BlockSpec(memory_space=pltpu.HBM)] * 3,
             out_specs=vmem,
             scratch_shapes=[
-                pltpu.VMEM((kept, chans, half), jnp.bfloat16),
+                pltpu.VMEM((chans, windows, half), jnp.bfloat16),
+                pltpu.VMEM((chans, nodes), jnp.int32),
+                pltpu.VMEM((chans, windows, half), jnp.bfloat16),
+                pltpu.VMEM((2 * BAND // 128, chans * windows, 128), jnp.float32),
                 pltpu.VMEM((STEP, BAND + FB), jnp.float32),
                 pltpu.VMEM((STEP, BAND + FB), jnp.float32),
                 pltpu.VMEM(((BAND + FB) // 128, half // STEP, 128), jnp.float32),
@@ -345,6 +366,8 @@
                 pltpu.SemaphoreType.DMA,
                 pltpu.SemaphoreType.DMA,
                 pltpu.SemaphoreType.DMA,
+                pltpu.SemaphoreType.DMA,
+                pltpu.SemaphoreType.DMA,
                 pltpu.SemaphoreType.DMA((n_chan,)),
                 pltpu.SemaphoreType.DMA((n_chan,)),
                 pltpu.SemaphoreType.REGULAR((n_chan.bit_length() - 1,)),
@@ -352,7 +375,7 @@
             compiler_params=pltpu.CompilerParams(
                 collective_id=0, has_side_effects=True, vmem_limit_bytes=16 * 1024 * 1024 + 4 * chans * nodes * FB
             ),
-        )(by_window, delays.T, offsets)
+        )(*(pltpu.with_memory_space_constraint(a, pltpu.HBM) for a in (traces, delays.T, offsets)))
 
     placed = (P("chan", None, "tm"), P(None, "chan"), P("tm"))
     return jax.shard_map(

time: 19.8 us -> 21 us (1.061)
  Pallas kernels: 17.3 us -> 20.3 us
  local copies, waits for them, and re-layouts: 2.3 us -> 0.61 us
    pallas_call x1, Pallas kernels: 17.3 us -> 20.3 us  [on_device(): pl.pallas_call(functools.partial(kernel, n_chan), out_shape=jax.ShapeDtyp...]
    unnamed x6 -> x1, local copies, waits for them, and re-layouts: 2.3 us -> 0.61 us
where the time goes in v4:
time: 21 us; the launch traced here: 20.9 us
  Pallas kernels  20.3 us (97%)
  local copies, waits for them, and re-layouts  0.61 us (3%)
    pallas_call x1, Pallas kernels, on_device(): pl.pallas_call(functools.partial(kernel, n_chan), out_shape=jax.ShapeDtyp...  20.3 us
    unnamed x1, local copies, waits for them, and re-layouts  0.61 us

profile of v4, /device:TPU:0, one launch (start us, length us, event | category | flops | bytes accessed | tf_op | source)
XLA Modules:
  0.0 20.9 jit_solution(14140804180550249589)
XLA Ops:
  0.0 20.3 %shard_map.37 = f32[2,8,256]{2,1,0:T(8,128)S(1)} custom-call(bf16[32,4,1024]{2,1,0:T(4,128)(2,1)} %x_hbm.1, s32[32,128]{1,0:T(8,128)} %bitcast.1, s32[2]{0:T(128)} %off_hbm.1), custom_call_target="tpu_custom_call" | custom-call | tf_op jit(solution)/shard_map/pallas_call | solution.py:340
  20.3 0.6 %copy.5 = f32[2,8,256]{2,1,0:T(8,128)} copy(f32[2,8,256]{2,1,0:T(8,128)S(1)} %shard_map.37) | data formatting | bytes 32768

commit v5 on v3

--- a/solution.py
+++ b/solution.py
@@ -60,21 +60,23 @@
 
 
 def kernel(
-    n_chan, x_ref, d_ref, off_hbm, out_ref,
-    other, base_c, base_s, lead_c, lead_s, fwd, inv, env, phase_c, phase_s,
+    n_chan, x_ref, d_hbm, off_hbm, out_ref,
+    d_ref, other, base_c, base_s, lead_c, lead_s, fwd, inv, env, phase_c, phase_s,
     nodes_d, turn_tab, turn_row, e_tab, send_buf, recv_buf,
-    off_ref, off_sem, x_send, x_recv, send_sem, recv_sem, round_sem,
+    off_ref, off_sem, d_sem, x_send, x_recv, send_sem, recv_sem, round_sem,
 ):
     windows, chans, half = x_ref.shape
     kept = windows // 2
     rows = kept * chans
-    nodes = d_ref.shape[1]
+    nodes = d_hbm.shape[1]
     node_rows = nodes // n_chan
     me = lax.axis_index("chan")
     tm = lax.axis_index("tm")
     partner = 1 - tm
 
     offsets_in = pltpu.make_async_copy(off_hbm, off_ref, off_sem)
+    delays_in = pltpu.make_async_copy(d_hbm, d_ref, d_sem)
+    delays_in.start()
     offsets_in.start()
 
     rounds = n_chan.bit_length() - 1
@@ -150,6 +152,7 @@
 
     hear(0)
 
+    delays_in.wait()
     nodes_d[...] = (d_ref[...].astype(jnp.float32) * unit).T
     block = PAIR * node_rows
     env_bins = 1.0 + float_iota((1, FB), 1)
@@ -175,13 +178,6 @@
 
     pl.loop(0, ahead)(phases)
     hear(1)
-    c, s = cos_sin((1.0 + float_iota((FB, TB), 0)) * (float_iota((FB, TB), 1) * (DEC * unit)))
-    turn_tab[:FB, :] = c
-    turn_tab[FB:, :] = -s
-    offsets_in.wait()
-    for w in range(kept):
-        shift = off_ref[w].astype(jnp.float32) * unit
-        turn_row[w, :, :FB], turn_row[w, :, FB:] = cos_sin(env_bins * shift)
     hear(2)
 
     own = x_ref[pl.ds(tm * kept, kept)].reshape(rows, half)
@@ -268,6 +264,14 @@
 
     send_pair(pairs - 1)
 
+    c, s = cos_sin((1.0 + float_iota((FB, TB), 0)) * (float_iota((FB, TB), 1) * (DEC * unit)))
+    turn_tab[:FB, :] = c
+    turn_tab[FB:, :] = -s
+    offsets_in.wait()
+    for w in range(kept):
+        shift = off_ref[w].astype(jnp.float32) * unit
+        turn_row[w, :, :FB], turn_row[w, :, FB:] = cos_sin(env_bins * shift)
+
     def incoming(source):
         return pltpu.make_async_remote_copy(
             src_ref=send_buf.at[source],
@@ -322,9 +326,10 @@
         return pl.pallas_call(
             functools.partial(kernel, n_chan),
             out_shape=jax.ShapeDtypeStruct((kept, node_rows, TB), jnp.float32),
-            in_specs=[vmem, vmem, pl.BlockSpec(memory_space=pltpu.HBM)],
+            in_specs=[vmem] + [pl.BlockSpec(memory_space=pltpu.HBM)] * 2,
             out_specs=vmem,
             scratch_shapes=[
+                pltpu.VMEM((chans, nodes), jnp.int32),
                 pltpu.VMEM((kept, chans, half), jnp.bfloat16),
                 pltpu.VMEM((STEP, BAND + FB), jnp.float32),
                 pltpu.VMEM((STEP, BAND + FB), jnp.float32),
@@ -345,6 +350,7 @@
                 pltpu.SemaphoreType.DMA,
                 pltpu.SemaphoreType.DMA,
                 pltpu.SemaphoreType.DMA,
+                pltpu.SemaphoreType.DMA,
                 pltpu.SemaphoreType.DMA((n_chan,)),
                 pltpu.SemaphoreType.DMA((n_chan,)),
                 pltpu.SemaphoreType.REGULAR((n_chan.bit_length() - 1,)),
@@ -352,7 +358,7 @@
             compiler_params=pltpu.CompilerParams(
                 collective_id=0, has_side_effects=True, vmem_limit_bytes=16 * 1024 * 1024 + 4 * chans * nodes * FB
             ),
-        )(by_window, delays.T, offsets)
+        )(by_window, *(pltpu.with_memory_space_constraint(a, pltpu.HBM) for a in (delays.T, offsets)))
 
     placed = (P("chan", None, "tm"), P(None, "chan"), P("tm"))
     return jax.shard_map(

time: 19.8 us -> 19.1 us (0.965)
  local copies, waits for them, and re-layouts: 2.3 us -> 1.64 us
    unnamed x6 -> x2, local copies, waits for them, and re-layouts: 2.3 us -> 1.64 us
where the time goes in v5:
time: 19.1 us; the launch traced here: 19 us
  Pallas kernels  17.4 us (91%)
  local copies, waits for them, and re-layouts  1.64 us (9%)
    pallas_call x1, Pallas kernels, on_device(): pl.pallas_call(functools.partial(kernel, n_chan), out_shape=jax.ShapeDtyp...  17.4 us
    unnamed x2, local copies, waits for them, and re-layouts  1.64 us

profile of v5, /device:TPU:0, one launch (start us, length us, event | category | flops | bytes accessed | tf_op | source)
XLA Modules:
  0.0 19.0 jit_solution(8077747722375651937)
XLA Ops:
  0.0 1.0 %copy.6 = bf16[32,4,1024]{2,0,1:T(8,128)(2,1)S(1)} copy(bf16[32,4,1024]{2,1,0:T(4,128)(2,1)} %param.3) | data formatting | bytes 524288 | tf_op args[0]
  1.0 17.4 %shard_map.37 = f32[2,8,256]{2,1,0:T(8,128)S(1)} custom-call(bf16[4,32,1024]{2,1,0:T(8,128)(2,1)S(1)} %bitcast.4, s32[32,128]{1,0:T(8,128)} %bitcast.5, s32[2]{0:T(128)} %off_hbm.1), custom_call_target="tpu_custom_call" | custom-call | tf_op jit(solution)/shard_map/pallas_call | solution.py:326
  18.4 0.6 %copy.8 = f32[2,8,256]{2,1,0:T(8,128)} copy(f32[2,8,256]{2,1,0:T(8,128)S(1)} %shard_map.37) | data formatting | bytes 32768
